TPU v7x, 32 devices: a whole 2x2x4 slice. The times are simulated.
32 devices in a mesh: cell: 4 (over z), spot: 8 (over y, x, core).
Axes of the slice: x: 2, y: 2, z: 4, core: 2. Of those that a mesh axis runs over, the one named last changes fastest.
Arguments:
- logits: float32 [4096, 4096], P('cell', 'spot'), may hold values from -4 to 330
- first_moment: bfloat16 [4096, 4096], P('cell', 'spot'), may hold values from -3 to 3
- second_moment: bfloat16 [4096, 4096], P('cell', 'spot'), may hold values from 0.049804688 to 1
- cell_expr: bfloat16 [4096, 128], P('cell'), may hold values from -36 to 36
- spot_expr: float32 [4096, 128], P('spot'), may hold values from -500 to 500
Outputs:
- new_logits: float32 [4096, 4096], P('cell', 'spot')
- new_first_moment: bfloat16 [4096, 4096], P('cell', 'spot')
- new_second_moment: bfloat16 [4096, 4096], P('cell', 'spot')
All inputs are finite; a program needn't handle non-finite values.
Results may differ from a plain program's by a relative error of at most 0.0052.
Values may be sent and summed in bfloat16 or wider, within the bound.
A program may use at most 64 MiB of HBM per device.

v0:
```python
import jax
import jax.numpy as jnp
from jax import lax
from jax.sharding import PartitionSpec as P

beta_one = 0.9
beta_two = 0.99
learn_rate = 0.1
adam_epsilon = 1e-08
norm_epsilon = 1e-06
adam_count = 10


def joined(value, axis, join):
    pieces = jax.tree.map(lambda part: lax.all_gather(part, axis), value)
    head = jax.tree.map(lambda part: part[0], pieces)
    tail = jax.tree.map(lambda part: part[1:], pieces)
    running, _ = lax.scan(lambda running, piece: (join(running, piece), None), head, tail)
    return running


def spot_term(predicted, target):
    spot_dot = jnp.sum(predicted * target, axis=1, keepdims=True)
    spot_pred = jnp.sum(predicted * predicted, axis=1, keepdims=True)
    spot_target = jnp.sum(target * target, axis=1, keepdims=True)
    return (target - spot_dot / (spot_pred + norm_epsilon) * predicted) / jnp.sqrt(
        (spot_pred + norm_epsilon) * (spot_target + norm_epsilon)
    )


def gene_partials(predicted, target):
    return (
        jnp.sum(predicted * target, axis=0),
        jnp.sum(predicted * predicted, axis=0),
        jnp.sum(target * target, axis=0),
    )


def gene_term(predicted, target, gene_dot, gene_pred, gene_target):
    gene_dot = gene_dot[None, :]
    gene_pred = gene_pred[None, :]
    gene_target = gene_target[None, :]
    return (target - gene_dot / (gene_pred + norm_epsilon) * predicted) / jnp.sqrt(
        (gene_pred + norm_epsilon) * (gene_target + norm_epsilon)
    )


def body(logits, first_moment, second_moment, cell_expr, spot_expr):
    cells = logits.shape[0] * lax.axis_size("cell")
    spots = logits.shape[1] * lax.axis_size("spot")
    genes = cell_expr.shape[1]
    loss_weight = jnp.sqrt(jnp.float32(genes * cells))
    ratio = spots / genes
    local_max = jnp.max(logits, axis=1)
    local_expo = jnp.exp(logits - local_max[:, None])
    local_total = jnp.sum(local_expo, axis=1)

    def combine(earlier, later):
        larger = jnp.maximum(earlier[0], later[0])
        return (
            larger,
            earlier[1] * jnp.exp(earlier[0] - larger) + later[1] * jnp.exp(later[0] - larger),
        )

    row_max, row_total = joined((local_max, local_total), "spot", combine)
    probs = local_expo * (jnp.exp(local_max - row_max) / row_total)[:, None]
    weights = probs.astype(jnp.bfloat16)
    partial_value = jnp.einsum("cs,cg->sg", weights, cell_expr, preferred_element_type=jnp.float32)
    predicted = lax.psum(partial_value, "cell")
    gene_dot, gene_pred, gene_target = lax.psum(gene_partials(predicted, spot_expr), "spot")
    pred_grad = -loss_weight * (
        spot_term(predicted, spot_expr)
        + ratio * gene_term(predicted, spot_expr, gene_dot, gene_pred, gene_target)
    )
    grad_rounded = pred_grad.astype(jnp.bfloat16)
    prob_grad = jnp.einsum("cg,sg->cs", cell_expr, grad_rounded, preferred_element_type=jnp.float32)
    row_dot = lax.psum(jnp.sum(probs * prob_grad, axis=1), "spot")
    logit_grad = probs * (prob_grad - row_dot[:, None])
    first_new = beta_one * first_moment.astype(jnp.float32) + (1.0 - beta_one) * logit_grad
    second_new = (
        beta_two * second_moment.astype(jnp.float32) + (1.0 - beta_two) * logit_grad * logit_grad
    )
    first_hat = first_new / (1.0 - beta_one**adam_count)
    second_hat = second_new / (1.0 - beta_two**adam_count)
    stepped = logits - learn_rate * first_hat / (jnp.sqrt(second_hat) + adam_epsilon)
    return (stepped, first_new.astype(jnp.bfloat16), second_new.astype(jnp.bfloat16))


def solution(mesh):
    placed = (
        P("cell", "spot"),
        P("cell", "spot"),
        P("cell", "spot"),
        P("cell", None),
        P("spot", None),
    )
    return jax.shard_map(
        body,
        mesh=mesh,
        in_specs=placed,
        out_specs=(P("cell", "spot"), P("cell", "spot"), P("cell", "spot")),
        check_vma=False,
    )
```

profile of v0, /device:TPU:0, one launch (start us, length us, event | category | flops | bytes accessed | tf_op | source)
XLA Modules:
  0.0 115.3 jit_solution(10364391293943496952)
XLA Ops:
  7.2 0.0 copy-start
  7.2 0.0 all-reduce.3.cloned.1.call-start
  7.2 2.0 %copy.18 = f32[1024,512]{0,1:T(8,128)S(1)} copy(f32[1024,512]{1,0:T(8,128)} %param.7) | data formatting | bytes 4194304 | tf_op args[0]
  9.2 1.8 %reduce_max.9 = f32[1024]{0:T(1024)S(1)} reduce(f32[1024,512]{1,0:T(8,128)} %param.7, f32[]{:T(128)} %constant.8.clone.1), dimensions={1}, to_apply=%region_0.0 | reduce | flops 523264 | bytes 2101252 | tf_op jit(solution)/shard_map/reduce_max | solution.py:54
  11.0 0.3 fusion.4
  11.3 10.6 %all-gather.1 = f32[8192]{0:T(1024)S(1)} all-gather(f32[1024]{0:T(1024)S(1)} %fusion.4), channel_id=3, replica_groups=mesh['cell'=4,'spot'=8] {'spot'}, dimensions={0}, use_global_device_ids=true | all-gather | bytes 36864 | tf_op jit(solution)/shard_map/all_gather | solution.py:15
  21.9 9.1 %all-gather = f32[8192]{0:T(1024)S(1)} all-gather(f32[1024]{0:T(1024)S(1)} %reduce_max.9), channel_id=2, replica_groups=mesh['cell'=4,'spot'=8] {'spot'}, dimensions={0}, use_global_device_ids=true | all-gather | bytes 36864 | tf_op jit(solution)/shard_map/all_gather | solution.py:15
  31.0 0.4 while.12
  31.4 0.0 copy-done
  31.4 1.2 %fusion.8 = f32[512,128]{1,0:T(8,128)} fusion(bf16[1024,128]{1,0:T(8,128)(2,1)S(1)} %copy-done, f32[1024,512]{0,1:T(8,128)S(1)} %copy.18, f32[1024]{0:T(1024)S(1)} %exponential_divide_fusion, f32[1024]{0:T(1024)S(1)} %reduce_max.9), kind=kOutput, calls=%fused_computation.17 | convolution fusion | flops 135790592 | bytes 2629632 | tf_op jit(solution)/shard_map/cs,cg->sg/dot_general | solution.py:68
  32.6 0.0 all-reduce.3.cloned.1.call-update
  32.6 1.5 %copy.15 = bf16[1024,512]{0,1:T(8,128)(2,1)S(1)} copy(bf16[1024,512]{1,0:T(8,128)(2,1)} %param.8) | data formatting | bytes 2097152 | tf_op args[1]
  34.1 2.3 %copy.17 = bf16[1024,512]{0,1:T(8,128)(2,1)} copy(bf16[1024,512]{1,0:T(8,128)(2,1)} %param.9) | data formatting | bytes 2097152 | tf_op args[2]
  36.4 32.3 %all-reduce.3.cloned.1.call-done = f32[512,128]{1,0:T(8,128)} async-done(((f32[512,128]{1,0:T(8,128)}), f32[512,128]{1,0:T(8,128)}) %all-reduce.3.cloned.1.call-update) | async-done | bytes 262160 | tf_op jit(solution)/shard_map/psum | solution.py:69
  68.6 1.3 %multiply_reduce_fusion.5 = (f32[512]{0:T(512)S(1)}, f32[128]{0:T(128)S(1)}, f32[128]{0:T(128)S(1)}, f32[512]{0:T(512)S(1)}, f32[128]{0:T(128)S(1)}, /*index=5*/f32[512]{0:T(512)S(1)}) fusion(f32[512,128]{1,0:T(8,128)} %all-reduce.3.cloned.1.call-done, f32[512,128]{1,0:T(8,128)} %param.11), kind=kLoop, calls=%fused_computation.33 | loop fusion | flops 587904 | bytes 531968 | tf_op jit(solution)/shard_map/reduce_sum | solution.py:23
  70.0 11.8 %all-reduce = (f32[128]{0:T(128)S(1)}, f32[128]{0:T(128)S(1)}, f32[128]{0:T(128)S(1)}) all-reduce(f32[128]{0:T(128)S(1)} %get-tuple-element.41, f32[128]{0:T(128)S(1)} %get-tuple-element.43, f32[128]{0:T(128)S(1)} %get-tuple-element.40), channel_id=1, replica_groups=mesh['cell'=4,'spot'=8] {'spot'}, use_global_device_ids=true, to_apply=%region_13.14 | all-reduce | flops 384 | bytes 3072 | tf_op jit(solution)/shard_map/psum | solution.py:70
  81.8 2.9 %fusion.1 = (f32[1024]{0:T(1024)S(1)}, f32[512,1024]{1,0:T(8,128)}) fusion(f32[1024,512]{0,1:T(8,128)S(1)} %copy.18, f32[1024]{0:T(1024)S(1)} %exponential_divide_fusion, f32[1024]{0:T(1024)S(1)} %reduce_max.9, bf16[1024,128]{1,0:T(8,128)(2,1)S(1)} %copy-done, f32[512,128]{1,0:T(8,128)} %param.11, f32[512,128]{1,0:T(8,128)} %all-reduce.3.cloned.1.call-done, ...), kind=kOutput, calls=%fused_computation.7 | convolution fusion | flops 136969216 | bytes 4998144 | tf_op jit(solution)/shard_map/cg,sg->cs/dot_general | solution.py:76
  84.7 11.8 %psum.39 = f32[1024]{0:T(1024)S(1)} all-reduce(f32[1024]{0:T(1024)S(1)} %get-tuple-element.69), channel_id=1, replica_groups=mesh['cell'=4,'spot'=8] {'spot'}, use_global_device_ids=true, to_apply=%region_15.16 | all-reduce | flops 1024 | bytes 8192 | tf_op jit(solution)/shard_map/psum | solution.py:77
  96.5 6.3 %fusion.7 = (bf16[1024,512]{0,1:T(8,128)(2,1)}, f32[1024,512]{0,1:T(8,128)}, bf16[1024,512]{0,1:T(8,128)(2,1)}) fusion(bf16[1024,512]{0,1:T(8,128)(2,1)} %copy.17, f32[1024]{0:T(1024)S(1)} %psum.39, f32[512,1024]{1,0:T(8,128)} %get-tuple-element.70, f32[1024]{0:T(1024)S(1)} %exponential_divide_fusion, f32[1024,512]{0,1:T(8,128)S(1)} %copy.18, ...), kind=kLoop, calls=%fused_computation.16 | loop fusion | flops 10485760 | bytes 10498048 | tf_op jit(solution)/shard_map/convert_element_type | solution.py:86
  102.9 0.0 copy-start.2
  102.9 3.0 %copy.19 = f32[1024,512]{1,0:T(8,128)} copy(f32[1024,512]{0,1:T(8,128)} %get-tuple-element.63) | data formatting | bytes 4194304
  105.8 0.0 copy-start.1
  105.8 0.0 copy-done.2
  105.9 1.3 %copy.20 = bf16[1024,512]{1,0:T(8,128)(2,1)} copy(bf16[1024,512]{0,1:T(8,128)(2,1)S(1)} %copy-done.2) | data formatting | bytes 2097152
  107.2 0.0 copy-done.1
  107.2 1.3 %copy.21 = bf16[1024,512]{1,0:T(8,128)(2,1)} copy(bf16[1024,512]{0,1:T(8,128)(2,1)S(1)} %copy-done.1) | data formatting | bytes 2097152
  (23 shorter events, 0.2 us)
Async XLA Ops:
  7.2 24.2 %copy-start = (bf16[1024,128]{1,0:T(8,128)(2,1)S(1)}, bf16[1024,128]{1,0:T(8,128)(2,1)}, u32[]{:S(2)}) copy-start(bf16[1024,128]{1,0:T(8,128)(2,1)} %param.10) | copy-start | bytes 786436
  7.2 61.5 %all-reduce.3.cloned.1.call-start = ((), (), s32[]{:S(2)}) async-start(), calls=%async_computation | async-start | bytes 524288 | tf_op jit(solution)/shard_map/psum | solution.py:69
  102.9 3.0 %copy-start.2 = (bf16[1024,512]{0,1:T(8,128)(2,1)S(1)}, bf16[1024,512]{0,1:T(8,128)(2,1)}, u32[]{:S(2)}) copy-start(bf16[1024,512]{0,1:T(8,128)(2,1)} %get-tuple-element.64) | copy-start | bytes 3145732
  105.8 1.3 %copy-start.1 = (bf16[1024,512]{0,1:T(8,128)(2,1)S(1)}, bf16[1024,512]{0,1:T(8,128)(2,1)}, u32[]{:S(2)}) copy-start(bf16[1024,512]{0,1:T(8,128)(2,1)} %get-tuple-element.62) | copy-start | bytes 3145732
Sparse Core Ops, SparseCore 0:
  32.7 35.8 all-reduce.2
where the time goes:
time: 116 us; the launch traced here: 115 us
  blocking collectives  43.3 us (37%)
  waiting for transfers between devices  32.3 us (28%)
  between operations  14.1 us (12%)
  local copies, waits for them, and re-layouts  11.4 us (10%)
  other arithmetic  9.89 us (9%)
  matrix products  4.08 us (4%)
    psum x1, waiting for transfers between devices, body(): predicted = lax.psum(partial_value, 'cell')  32.3 us
    all_gather x2, blocking collectives, joined(): pieces = jax.tree.map(lambda part: lax.all_gather(part, axis), value)  19.7 us
    psum x1, blocking collectives, body(): lax.psum(gene_partials(predicted, spot_expr), 'spot')  11.8 us
    psum x1, blocking collectives, body(): row_dot = lax.psum(jnp.sum(probs * prob_grad, axis=1), 'spot')  11.8 us
    unnamed x12, local copies, waits for them, and re-layouts  11.3 us
    convert_element_type x1, other arithmetic, body(): second_new.astype(jnp.bfloat16)  6.33 us
    dot_general x1, matrix products, body(): jnp.einsum('cg,sg->cs', cell_expr, grad_rounded, preferred_element_type=j...  2.89 us
  transfers between devices with their start and end apart: 1, of which 1 were waited for; matrix products, arithmetic and copies ran while one was open for 3% of the time, Pallas kernels for 0%

commit v1 on v0

v1 whole, which is shorter than its diff:
```python
import functools

import jax
import jax.numpy as jnp
from jax import lax
from jax.experimental import pallas as pl
from jax.experimental.pallas import tpu as pltpu
from jax.sharding import PartitionSpec as P

beta_one = 0.9
beta_two = 0.99
learn_rate = 0.1
adam_epsilon = 1e-08
norm_epsilon = 1e-06
adam_count = 10

MESH = pl.DeviceIdType.MESH
LANES = 128
WIRE = jnp.float32


def eye_mask():
    row = lax.broadcasted_iota(jnp.int32, (LANES, LANES), 0)
    lane = lax.broadcasted_iota(jnp.int32, (LANES, LANES), 1)
    return row == lane


def to_row(column, mask):
    wide = jnp.broadcast_to(column, (column.shape[0], LANES))
    return jnp.sum(jnp.where(mask[: column.shape[0]], wide, 0.0), axis=0, keepdims=True)


def to_column(row, mask, count=LANES):
    wide = jnp.broadcast_to(row, (count, LANES))
    return jnp.sum(jnp.where(mask[:count], wide, 0.0), axis=1, keepdims=True)


def exchange_kernel(
    cell_n, spot_n, cells, spots,
    logits_hbm, expr_hbm, target_hbm,
    stats_out, grad_out,
    logits, expr, target, probs, weights, expr_t, target_t, part,
    stat_mine, stat_peer, part_peer, spot_mine, spot_peer, gene_mine, gene_peer,
    grads, dots_mine, dots_peer,
    load_sem, stat_send, stat_recv, part_send, part_recv, sums_send, sums_recv,
    gene_send, gene_recv, grad_send, grad_recv, dots_send, dots_recv,
):
    rows, width = logits.shape
    genes = expr.shape[1]
    own_genes = genes // cell_n
    chunks = rows // LANES
    loss_weight = float(genes * cells) ** 0.5
    ratio = spots / genes
    my_cell = lax.axis_index("cell")
    my_spot = lax.axis_index("spot")

    def cell_peer(k):
        return (lax.rem(my_cell + k, cell_n), my_spot)

    def spot_peer_id(k):
        return (my_cell, lax.rem(my_spot + k, spot_n))

    loads = [
        pltpu.make_async_copy(
            logits_hbm.at[pl.ds(i * LANES, LANES)], logits.at[pl.ds(i * LANES, LANES)], load_sem.at[i]
        )
        for i in range(chunks)
    ]
    loads.append(pltpu.make_async_copy(expr_hbm, expr, load_sem.at[chunks]))
    loads.append(pltpu.make_async_copy(target_hbm, target, load_sem.at[chunks + 1]))
    for load in loads:
        load.start()
    barrier = pltpu.get_barrier_semaphore()
    for k in range(1, cell_n):
        pl.semaphore_signal(barrier, inc=1, device_id=cell_peer(k), device_id_type=MESH)
    for k in range(1, spot_n):
        pl.semaphore_signal(barrier, inc=1, device_id=spot_peer_id(k), device_id_type=MESH)

    mask = eye_mask()

    for i in range(chunks):
        loads[i].wait()
        block = logits[i * LANES : (i + 1) * LANES, :]
        top = jnp.max(block, axis=1, keepdims=True)
        expo = jnp.exp(block - top)
        probs[i * LANES : (i + 1) * LANES, :] = expo
        stat_mine[i : i + 1, :] = to_row(top, mask)
        stat_mine[chunks + i : chunks + i + 1, :] = to_row(
            jnp.sum(expo, axis=1, keepdims=True), mask
        )

    pl.semaphore_wait(barrier, cell_n + spot_n - 2)

    def send(src, dst, send_sem, recv_sem, device):
        copy = pltpu.make_async_remote_copy(
            src_ref=src, dst_ref=dst, send_sem=send_sem, recv_sem=recv_sem,
            device_id=device, device_id_type=MESH,
        )
        copy.start()
        return copy

    stat_copies = [
        send(stat_mine, stat_peer.at[k - 1], stat_send.at[k - 1], stat_recv.at[k - 1], spot_peer_id(k))
        for k in range(1, spot_n)
    ]
    loads[chunks].wait()
    loads[chunks + 1].wait()
    expr_t[...] = expr[...].astype(jnp.float32).T.astype(jnp.bfloat16)
    flipped = target[...].T
    target_t[...] = flipped.reshape(target_t.shape)
    spot_target = jnp.sum(flipped * flipped, axis=0, keepdims=True)
    own_target = target_t[my_cell]
    gene_mine[2:3, :] = to_row(jnp.sum(own_target * own_target, axis=1, keepdims=True), mask)
    for copy in stat_copies:
        copy.wait()

    local_max = stat_mine[:chunks, :]
    row_max = local_max
    for k in range(spot_n - 1):
        row_max = jnp.maximum(row_max, stat_peer[k, :chunks, :])
    row_total = stat_mine[chunks:, :] * jnp.exp(local_max - row_max)
    for k in range(spot_n - 1):
        row_total = row_total + stat_peer[k, chunks:, :] * jnp.exp(stat_peer[k, :chunks, :] - row_max)
    factor = jnp.exp(local_max - row_max) / row_total
    stats_out[:chunks, :] = row_max
    stats_out[chunks : 2 * chunks, :] = 1.0 / row_total
    for i in range(chunks):
        part_rows = slice(i * LANES, (i + 1) * LANES)
        prob = probs[part_rows, :] * to_column(factor[i : i + 1, :], mask)
        probs[part_rows, :] = prob
        weights[part_rows, :] = prob.astype(jnp.bfloat16)
    partial = jnp.dot(expr_t[...], weights[...], preferred_element_type=jnp.float32)
    part[...] = partial.astype(part.dtype).reshape(part.shape)

    part_copies = [
        send(part.at[lax.rem(my_cell + k, cell_n)], part_peer.at[k - 1], part_send.at[k - 1],
             part_recv.at[k - 1], cell_peer(k))
        for k in range(1, cell_n)
    ]
    for copy in part_copies:
        copy.wait()
    predicted = part[my_cell].astype(jnp.float32)
    for k in range(cell_n - 1):
        predicted = predicted + part_peer[k].astype(jnp.float32)

    product = predicted * own_target
    square = predicted * predicted
    spot_mine[0:1, :] = jnp.sum(product, axis=0, keepdims=True)
    spot_mine[1:2, :] = jnp.sum(square, axis=0, keepdims=True)
    spot_copies = [
        send(spot_mine, spot_peer.at[k - 1], sums_send.at[k - 1], sums_recv.at[k - 1], cell_peer(k))
        for k in range(1, cell_n)
    ]
    gene_mine[0:1, :] = to_row(jnp.sum(product, axis=1, keepdims=True), mask)
    gene_mine[1:2, :] = to_row(jnp.sum(square, axis=1, keepdims=True), mask)
    gene_copies = [
        send(gene_mine, gene_peer.at[k - 1], gene_send.at[k - 1], gene_recv.at[k - 1], spot_peer_id(k))
        for k in range(1, spot_n)
    ]
    for copy in gene_copies:
        copy.wait()
    gene_sums = gene_mine[...]
    for k in range(spot_n - 1):
        gene_sums = gene_sums + gene_peer[k]
    gene_scale = lax.rsqrt((gene_sums[1:2] + norm_epsilon) * (gene_sums[2:3] + norm_epsilon))
    gene_lean = gene_sums[0:1] / (gene_sums[1:2] + norm_epsilon)
    gene_scale = to_column(gene_scale, mask, own_genes)
    gene_lean = to_column(gene_lean, mask, own_genes)
    by_gene = (own_target - gene_lean * predicted) * gene_scale
    for copy in spot_copies:
        copy.wait()
    spot_sums = spot_mine[...]
    for k in range(cell_n - 1):
        spot_sums = spot_sums + spot_peer[k]
    spot_scale = lax.rsqrt((spot_sums[1:2] + norm_epsilon) * (spot_target + norm_epsilon))
    spot_lean = spot_sums[0:1] / (spot_sums[1:2] + norm_epsilon)
    by_spot = (own_target - spot_lean * predicted) * spot_scale
    grad = -loss_weight * (by_spot + ratio * by_gene)
    grads[my_cell] = grad.astype(jnp.bfloat16)
    grad_copies = [
        send(grads.at[my_cell], grads.at[my_cell], grad_send.at[k - 1], grad_recv.at[k - 1], cell_peer(k))
        for k in range(1, cell_n)
    ]
    for copy in grad_copies:
        copy.wait()
    grad_all = grads[...].reshape(genes, width)
    grad_out[...] = grad_all
    for i in range(chunks):
        part_rows = slice(i * LANES, (i + 1) * LANES)
        prob_grad = jnp.dot(expr[part_rows, :], grad_all, preferred_element_type=jnp.float32)
        dots_mine[i : i + 1, :] = to_row(
            jnp.sum(probs[part_rows, :] * prob_grad, axis=1, keepdims=True), mask
        )
    dots_copies = [
        send(dots_mine, dots_peer.at[k - 1], dots_send.at[k - 1], dots_recv.at[k - 1], spot_peer_id(k))
        for k in range(1, spot_n)
    ]
    for copy in dots_copies:
        copy.wait()
    row_dot = dots_mine[...]
    for k in range(spot_n - 1):
        row_dot = row_dot + dots_peer[k]
    stats_out[2 * chunks :, :] = row_dot


def update_kernel(
    chunks, stats, grad, logits, first, second, expr, new_logits, new_first, new_second
):
    at = pl.program_id(0)
    mask = eye_mask()
    per = logits.shape[0] // LANES
    for j in range(per):
        span = slice(j * LANES, (j + 1) * LANES)
        row = at * per + j
        row_max = to_column(stats[pl.ds(row, 1), :], mask)
        scale = to_column(stats[pl.ds(chunks + row, 1), :], mask)
        row_dot = to_column(stats[pl.ds(2 * chunks + row, 1), :], mask)
        block = logits[span, :]
        prob = jnp.exp(block - row_max) * scale
        prob_grad = jnp.dot(expr[span, :], grad[...], preferred_element_type=jnp.float32)
        logit_grad = prob * (prob_grad - row_dot)
        first_new = beta_one * first[span, :].astype(jnp.float32) + (1.0 - beta_one) * logit_grad
        second_new = (
            beta_two * second[span, :].astype(jnp.float32)
            + (1.0 - beta_two) * logit_grad * logit_grad
        )
        first_hat = first_new * (learn_rate / (1.0 - beta_one**adam_count))
        second_hat = second_new * (1.0 / (1.0 - beta_two**adam_count))
        new_logits[span, :] = block - first_hat / (jnp.sqrt(second_hat) + adam_epsilon)
        new_first[span, :] = first_new.astype(jnp.bfloat16)
        new_second[span, :] = second_new.astype(jnp.bfloat16)


def body(cell_n, spot_n, logits, first_moment, second_moment, cell_expr, spot_expr):
    rows, width = logits.shape
    genes = cell_expr.shape[1]
    own_genes = genes // cell_n
    chunks = rows // LANES
    f32 = jnp.float32
    dma = pltpu.SemaphoreType.DMA
    anywhere = pl.BlockSpec(memory_space=pl.ANY)
    in_vmem = pl.BlockSpec(memory_space=pltpu.VMEM)
    cell_sem = dma((cell_n - 1,))
    spot_sem = dma((spot_n - 1,))
    stats, grad = pl.pallas_call(
        functools.partial(exchange_kernel, cell_n, spot_n, rows * cell_n, width * spot_n),
        out_shape=(
            jax.ShapeDtypeStruct((3 * chunks, LANES), f32),
            jax.ShapeDtypeStruct((genes, width), jnp.bfloat16),
        ),
        in_specs=[anywhere] * 3,
        out_specs=(in_vmem, in_vmem),
        scratch_shapes=[
            pltpu.VMEM((rows, width), f32),
            pltpu.VMEM((rows, genes), jnp.bfloat16),
            pltpu.VMEM((width, genes), f32),
            pltpu.VMEM((rows, width), f32),
            pltpu.VMEM((rows, width), jnp.bfloat16),
            pltpu.VMEM((genes, rows), jnp.bfloat16),
            pltpu.VMEM((cell_n, own_genes, width), f32),
            pltpu.VMEM((cell_n, own_genes, width), WIRE),
            pltpu.VMEM((2 * chunks, LANES), f32),
            pltpu.VMEM((spot_n - 1, 2 * chunks, LANES), f32),
            pltpu.VMEM((cell_n - 1, own_genes, width), WIRE),
            pltpu.VMEM((2, width), f32),
            pltpu.VMEM((cell_n - 1, 2, width), f32),
            pltpu.VMEM((3, LANES), f32),
            pltpu.VMEM((spot_n - 1, 3, LANES), f32),
            pltpu.VMEM((cell_n, own_genes, width), jnp.bfloat16),
            pltpu.VMEM((chunks, LANES), f32),
            pltpu.VMEM((spot_n - 1, chunks, LANES), f32),
            dma((chunks + 2,)),
            spot_sem, spot_sem, cell_sem, cell_sem, cell_sem, cell_sem,
            spot_sem, spot_sem, cell_sem, cell_sem, spot_sem, spot_sem,
        ],
        compiler_params=pltpu.CompilerParams(
            collective_id=0, has_side_effects=True, vmem_limit_bytes=32 << 20
        ),
        name="exchange",
    )(logits, cell_expr, spot_expr)
    tile = 2 * LANES if rows % (2 * LANES) == 0 else LANES
    by_row = pl.BlockSpec((tile, width), lambda i: (i, 0))
    return pl.pallas_call(
        functools.partial(update_kernel, chunks),
        grid=(rows // tile,),
        out_shape=(
            jax.ShapeDtypeStruct(logits.shape, f32),
            jax.ShapeDtypeStruct(logits.shape, jnp.bfloat16),
            jax.ShapeDtypeStruct(logits.shape, jnp.bfloat16),
        ),
        in_specs=[
            pl.BlockSpec(stats.shape, lambda i: (0, 0)),
            pl.BlockSpec(grad.shape, lambda i: (0, 0)),
            by_row,
            by_row,
            by_row,
            pl.BlockSpec((tile, genes), lambda i: (i, 0)),
        ],
        out_specs=(by_row, by_row, by_row),
        name="update",
    )(stats, grad, logits, first_moment, second_moment, cell_expr)


def solution(mesh):
    placed = (
        P("cell", "spot"),
        P("cell", "spot"),
        P("cell", "spot"),
        P("cell", None),
        P("spot", None),
    )
    return jax.shard_map(
        functools.partial(body, mesh.shape["cell"], mesh.shape["spot"]),
        mesh=mesh,
        in_specs=placed,
        out_specs=(P("cell", "spot"), P("cell", "spot"), P("cell", "spot")),
        check_vma=False,
    )
```

time: 116 us -> 40.6 us (0.35)
  blocking collectives: 43.3 us -> 0 us
  Pallas kernels: 0 us -> 35 us
  waiting for transfers between devices: 32.3 us -> 0 us
  between operations: 14.1 us -> 0.66 us
  other arithmetic: 9.89 us -> 0 us
  local copies, waits for them, and re-layouts: 11.4 us -> 4.72 us
  matrix products: 4.08 us -> 0 us
    pallas_call x0 -> x2, Pallas kernels: none -> 35 us  [the longest x1 29.1 us: body(): pl.pallas_call(functools.partial(exchange_kernel, cell_n, spot_n, rows *...]
    psum x1 -> x0, waiting for transfers between devices: 32.3 us -> none  [body(): predicted = lax.psum(partial_value, 'cell')]
    psum x2 -> x0, blocking collectives: 23.7 us -> none  [the longest x1 11.8 us: body(): lax.psum(gene_partials(predicted, spot_expr), 'spot')]
    all_gather x2 -> x0, blocking collectives: 19.7 us -> none  [joined(): pieces = jax.tree.map(lambda part: lax.all_gather(part, axis), value)]
    unnamed x12 -> x10, local copies, waits for them, and re-layouts: 11.3 us -> 4.72 us
    convert_element_type x1 -> x0, other arithmetic: 6.33 us -> none  [body(): second_new.astype(jnp.bfloat16)]
    dot_general x2 -> x0, matrix products: 4.08 us -> none  [the longest x1 2.89 us: body(): jnp.einsum('cg,sg->cs', cell_expr, grad_rounded, preferred_element_type=j...]
    reduce_max x1 -> x0, other arithmetic: 1.8 us -> none  [body(): local_max = jnp.max(logits, axis=1)]
  transfers between devices with their start and end apart: 1 -> 0, of which waited for: 1 -> 0; matrix products, arithmetic and copies ran while one was open for 3% -> 0% of each run, Pallas kernels for 0% -> 0%
where the time goes in v1:
time: 40.6 us; the launch traced here: 40.3 us
  Pallas kernels  35 us (86%)
  local copies, waits for them, and re-layouts  4.72 us (12%)
  between operations  0.66 us (2%)
    pallas_call x1, Pallas kernels, body(): pl.pallas_call(functools.partial(exchange_kernel, cell_n, spot_n, rows *...  29.1 us
    pallas_call x1, Pallas kernels, body(): pl.pallas_call(functools.partial(update_kernel, chunks), grid=(rows // ti...  5.89 us
    unnamed x10, local copies, waits for them, and re-layouts  4.72 us

profile of v1, /device:TPU:0, one launch (start us, length us, event | category | flops | bytes accessed | tf_op | source)
XLA Modules:
  0.0 40.3 jit_solution(14486054685346317119)
XLA Ops:
  0.6 0.0 copy-start
  0.6 1.6 %copy-done = f32[1024,512]{1,0:T(8,128)S(1)} copy-done((f32[1024,512]{1,0:T(8,128)S(1)}, f32[1024,512]{1,0:T(8,128)}, u32[]{:S(2)}) %copy-start) | copy-done | bytes 2097176
  2.2 0.0 copy-start.1
  2.2 0.9 %copy-done.1 = bf16[1024,128]{1,0:T(8,128)(2,1)S(1)} copy-done((bf16[1024,128]{1,0:T(8,128)(2,1)S(1)}, bf16[1024,128]{1,0:T(8,128)(2,1)}, u32[]{:S(2)}) %copy-start.1) | copy-done | bytes 262168
  3.2 0.0 copy-start.2
  3.2 0.9 %copy-done.2 = f32[512,128]{1,0:T(8,128)S(1)} copy-done((f32[512,128]{1,0:T(8,128)S(1)}, f32[512,128]{1,0:T(8,128)}, u32[]{:S(2)}) %copy-start.2) | copy-done | bytes 262168
  4.1 29.1 %exchange.1 = (f32[24,128]{1,0:T(8,128)S(1)}, bf16[128,512]{1,0:T(8,128)(2,1)S(1)}) custom-call(f32[1024,512]{1,0:T(8,128)S(1)} %copy-done, bf16[1024,128]{1,0:T(8,128)(2,1)S(1)} %copy-done.1, f32[512,128]{1,0:T(8,128)S(1)} %copy-done.2), custom_call_target="tpu_custom_call" | custom-call | tf_op jit(solution)/shard_map/exchange/pallas_call | solution.py:245
  33.2 0.0 copy-start.3
  33.2 0.6 %copy-done.3 = bf16[128,512]{1,0:T(8,128)(2,1)} copy-done((bf16[128,512]{1,0:T(8,128)(2,1)}, bf16[128,512]{1,0:T(8,128)(2,1)S(1)}, u32[]{:S(2)}) %copy-start.3) | copy-done | bytes 131096
  33.8 0.0 copy-start.4
  33.8 0.6 %copy-done.4 = f32[24,128]{1,0:T(8,128)} copy-done((f32[24,128]{1,0:T(8,128)}, f32[24,128]{1,0:T(8,128)S(1)}, u32[]{:S(2)}) %copy-start.4) | copy-done | bytes 12312
  34.4 5.9 %update.1 = (f32[1024,512]{1,0:T(8,128)}, bf16[1024,512]{1,0:T(8,128)(2,1)}, bf16[1024,512]{1,0:T(8,128)(2,1)}) custom-call(f32[24,128]{1,0:T(8,128)} %copy-done.4, bf16[128,512]{1,0:T(8,128)(2,1)} %copy-done.3, f32[1024,512]{1,0:T(8,128)} %logits.1, bf16[1024,512]{1,0:T(8,128)(2,1)} %first.1, bf16[1024,512]{1,0:T(8,128)(2,1)} %second.1, bf16[1024,128]{1,0:T(8,128)(2,1)} %expr.1), custom_call_target="tpu_custom_call" | custom-call | tf_op jit(solution)/shard_map/update/pallas_call | solution.py:283
Async XLA Ops:
  0.6 1.6 %copy-start = (f32[1024,512]{1,0:T(8,128)S(1)}, f32[1024,512]{1,0:T(8,128)}, u32[]{:S(2)}) copy-start(f32[1024,512]{1,0:T(8,128)} %logits.1) | copy-start | bytes 6291460
  2.2 0.9 %copy-start.1 = (bf16[1024,128]{1,0:T(8,128)(2,1)S(1)}, bf16[1024,128]{1,0:T(8,128)(2,1)}, u32[]{:S(2)}) copy-start(bf16[1024,128]{1,0:T(8,128)(2,1)} %expr.1) | copy-start | bytes 786436
  3.2 0.9 %copy-start.2 = (f32[512,128]{1,0:T(8,128)S(1)}, f32[512,128]{1,0:T(8,128)}, u32[]{:S(2)}) copy-start(f32[512,128]{1,0:T(8,128)} %target_hbm.1) | copy-start | bytes 786436
  33.2 0.6 %copy-start.3 = (bf16[128,512]{1,0:T(8,128)(2,1)}, bf16[128,512]{1,0:T(8,128)(2,1)S(1)}, u32[]{:S(2)}) copy-start(bf16[128,512]{1,0:T(8,128)(2,1)S(1)} %get-tuple-element.6.grad) | copy-start | bytes 393220
  33.8 0.6 %copy-start.4 = (f32[24,128]{1,0:T(8,128)}, f32[24,128]{1,0:T(8,128)S(1)}, u32[]{:S(2)}) copy-start(f32[24,128]{1,0:T(8,128)S(1)} %get-tuple-element.5.stats) | copy-start | bytes 36868

commit v2 on v1

--- a/solution.py
+++ b/solution.py
@@ -16,7 +16,7 @@
 
 MESH = pl.DeviceIdType.MESH
 LANES = 128
-WIRE = jnp.float32
+WIRE = jnp.bfloat16
 
 
 def eye_mask():
@@ -37,9 +37,9 @@
 
 def exchange_kernel(
     cell_n, spot_n, cells, spots,
-    logits_hbm, expr_hbm, target_hbm,
-    stats_out, grad_out,
-    logits, expr, target, probs, weights, expr_t, target_t, part,
+    logits_hbm, expr_hbm, target_hbm, first_hbm, second_hbm,
+    logits, first, second, probs, prob_grads, row_dots,
+    expr, target, weights, expr_t, target_t, own_part, part,
     stat_mine, stat_peer, part_peer, spot_mine, spot_peer, gene_mine, gene_peer,
     grads, dots_mine, dots_peer,
     load_sem, stat_send, stat_recv, part_send, part_recv, sums_send, sums_recv,
@@ -68,6 +68,8 @@
     ]
     loads.append(pltpu.make_async_copy(expr_hbm, expr, load_sem.at[chunks]))
     loads.append(pltpu.make_async_copy(target_hbm, target, load_sem.at[chunks + 1]))
+    loads.append(pltpu.make_async_copy(first_hbm, first, load_sem.at[chunks + 2]))
+    loads.append(pltpu.make_async_copy(second_hbm, second, load_sem.at[chunks + 3]))
     for load in loads:
         load.start()
     barrier = pltpu.get_barrier_semaphore()
@@ -122,8 +124,6 @@
     for k in range(spot_n - 1):
         row_total = row_total + stat_peer[k, chunks:, :] * jnp.exp(stat_peer[k, :chunks, :] - row_max)
     factor = jnp.exp(local_max - row_max) / row_total
-    stats_out[:chunks, :] = row_max
-    stats_out[chunks : 2 * chunks, :] = 1.0 / row_total
     for i in range(chunks):
         part_rows = slice(i * LANES, (i + 1) * LANES)
         prob = probs[part_rows, :] * to_column(factor[i : i + 1, :], mask)
@@ -131,6 +131,7 @@
         weights[part_rows, :] = prob.astype(jnp.bfloat16)
     partial = jnp.dot(expr_t[...], weights[...], preferred_element_type=jnp.float32)
     part[...] = partial.astype(part.dtype).reshape(part.shape)
+    own_part[...] = partial.reshape(own_part.shape)
 
     part_copies = [
         send(part.at[lax.rem(my_cell + k, cell_n)], part_peer.at[k - 1], part_send.at[k - 1],
@@ -139,7 +140,7 @@
     ]
     for copy in part_copies:
         copy.wait()
-    predicted = part[my_cell].astype(jnp.float32)
+    predicted = own_part[my_cell]
     for k in range(cell_n - 1):
         predicted = predicted + part_peer[k].astype(jnp.float32)
 
@@ -184,10 +185,10 @@
     for copy in grad_copies:
         copy.wait()
     grad_all = grads[...].reshape(genes, width)
-    grad_out[...] = grad_all
     for i in range(chunks):
         part_rows = slice(i * LANES, (i + 1) * LANES)
         prob_grad = jnp.dot(expr[part_rows, :], grad_all, preferred_element_type=jnp.float32)
+        prob_grads[part_rows, :] = prob_grad
         dots_mine[i : i + 1, :] = to_row(
             jnp.sum(probs[part_rows, :] * prob_grad, axis=1, keepdims=True), mask
         )
@@ -195,38 +196,36 @@
         send(dots_mine, dots_peer.at[k - 1], dots_send.at[k - 1], dots_recv.at[k - 1], spot_peer_id(k))
         for k in range(1, spot_n)
     ]
+    loads[chunks + 2].wait()
+    loads[chunks + 3].wait()
     for copy in dots_copies:
         copy.wait()
     row_dot = dots_mine[...]
     for k in range(spot_n - 1):
         row_dot = row_dot + dots_peer[k]
-    stats_out[2 * chunks :, :] = row_dot
+    row_dots[...] = row_dot
 
 
 def update_kernel(
-    chunks, stats, grad, logits, first, second, expr, new_logits, new_first, new_second
+    logits, first, second, probs, prob_grads, row_dots, new_logits, new_first, new_second
 ):
     at = pl.program_id(0)
     mask = eye_mask()
-    per = logits.shape[0] // LANES
+    per = new_logits.shape[0] // LANES
     for j in range(per):
         span = slice(j * LANES, (j + 1) * LANES)
         row = at * per + j
-        row_max = to_column(stats[pl.ds(row, 1), :], mask)
-        scale = to_column(stats[pl.ds(chunks + row, 1), :], mask)
-        row_dot = to_column(stats[pl.ds(2 * chunks + row, 1), :], mask)
-        block = logits[span, :]
-        prob = jnp.exp(block - row_max) * scale
-        prob_grad = jnp.dot(expr[span, :], grad[...], preferred_element_type=jnp.float32)
-        logit_grad = prob * (prob_grad - row_dot)
-        first_new = beta_one * first[span, :].astype(jnp.float32) + (1.0 - beta_one) * logit_grad
+        rows = pl.ds(pl.multiple_of(row * LANES, LANES), LANES)
+        row_dot = to_column(row_dots[pl.ds(row, 1), :], mask)
+        logit_grad = probs[rows, :] * (prob_grads[rows, :] - row_dot)
+        first_new = beta_one * first[rows, :].astype(jnp.float32) + (1.0 - beta_one) * logit_grad
         second_new = (
-            beta_two * second[span, :].astype(jnp.float32)
+            beta_two * second[rows, :].astype(jnp.float32)
             + (1.0 - beta_two) * logit_grad * logit_grad
         )
         first_hat = first_new * (learn_rate / (1.0 - beta_one**adam_count))
         second_hat = second_new * (1.0 / (1.0 - beta_two**adam_count))
-        new_logits[span, :] = block - first_hat / (jnp.sqrt(second_hat) + adam_epsilon)
+        new_logits[span, :] = logits[rows, :] - first_hat / (jnp.sqrt(second_hat) + adam_epsilon)
         new_first[span, :] = first_new.astype(jnp.bfloat16)
         new_second[span, :] = second_new.astype(jnp.bfloat16)
 
@@ -238,25 +237,23 @@
     chunks = rows // LANES
     f32 = jnp.float32
     dma = pltpu.SemaphoreType.DMA
-    anywhere = pl.BlockSpec(memory_space=pl.ANY)
+    in_hbm = pl.BlockSpec(memory_space=pltpu.HBM)
     in_vmem = pl.BlockSpec(memory_space=pltpu.VMEM)
     cell_sem = dma((cell_n - 1,))
     spot_sem = dma((spot_n - 1,))
-    stats, grad = pl.pallas_call(
+    like = [jax.ShapeDtypeStruct(x.shape, x.dtype) for x in (logits, first_moment, second_moment)]
+    operands = (logits, cell_expr, spot_expr, first_moment, second_moment)
+    held = pl.pallas_call(
         functools.partial(exchange_kernel, cell_n, spot_n, rows * cell_n, width * spot_n),
-        out_shape=(
-            jax.ShapeDtypeStruct((3 * chunks, LANES), f32),
-            jax.ShapeDtypeStruct((genes, width), jnp.bfloat16),
-        ),
-        in_specs=[anywhere] * 3,
-        out_specs=(in_vmem, in_vmem),
+        out_shape=(*like, like[0], like[0], jax.ShapeDtypeStruct((chunks, LANES), f32)),
+        in_specs=[in_hbm] * 5,
+        out_specs=(in_vmem,) * 6,
         scratch_shapes=[
-            pltpu.VMEM((rows, width), f32),
             pltpu.VMEM((rows, genes), jnp.bfloat16),
             pltpu.VMEM((width, genes), f32),
-            pltpu.VMEM((rows, width), f32),
             pltpu.VMEM((rows, width), jnp.bfloat16),
             pltpu.VMEM((genes, rows), jnp.bfloat16),
+            pltpu.VMEM((cell_n, own_genes, width), f32),
             pltpu.VMEM((cell_n, own_genes, width), f32),
             pltpu.VMEM((cell_n, own_genes, width), WIRE),
             pltpu.VMEM((2 * chunks, LANES), f32),
@@ -269,36 +266,29 @@
             pltpu.VMEM((cell_n, own_genes, width), jnp.bfloat16),
             pltpu.VMEM((chunks, LANES), f32),
             pltpu.VMEM((spot_n - 1, chunks, LANES), f32),
-            dma((chunks + 2,)),
+            dma((chunks + 4,)),
             spot_sem, spot_sem, cell_sem, cell_sem, cell_sem, cell_sem,
             spot_sem, spot_sem, cell_sem, cell_sem, spot_sem, spot_sem,
         ],
         compiler_params=pltpu.CompilerParams(
-            collective_id=0, has_side_effects=True, vmem_limit_bytes=32 << 20
+            collective_id=0, has_side_effects=True, vmem_limit_bytes=24 << 20
+        ),
+        cost_estimate=pl.CostEstimate(
+            flops=4 * rows * width * genes, bytes_accessed=32 * rows * width, transcendentals=rows * width
         ),
         name="exchange",
-    )(logits, cell_expr, spot_expr)
+    )(*(pltpu.with_memory_space_constraint(x, pltpu.HBM) for x in operands))
     tile = 2 * LANES if rows % (2 * LANES) == 0 else LANES
     by_row = pl.BlockSpec((tile, width), lambda i: (i, 0))
     return pl.pallas_call(
-        functools.partial(update_kernel, chunks),
+        update_kernel,
         grid=(rows // tile,),
-        out_shape=(
-            jax.ShapeDtypeStruct(logits.shape, f32),
-            jax.ShapeDtypeStruct(logits.shape, jnp.bfloat16),
-            jax.ShapeDtypeStruct(logits.shape, jnp.bfloat16),
-        ),
-        in_specs=[
-            pl.BlockSpec(stats.shape, lambda i: (0, 0)),
-            pl.BlockSpec(grad.shape, lambda i: (0, 0)),
-            by_row,
-            by_row,
-            by_row,
-            pl.BlockSpec((tile, genes), lambda i: (i, 0)),
-        ],
+        out_shape=like,
+        in_specs=[in_vmem] * 6,
         out_specs=(by_row, by_row, by_row),
+        compiler_params=pltpu.CompilerParams(vmem_limit_bytes=16 << 20),
         name="update",
-    )(stats, grad, logits, first_moment, second_moment, cell_expr)
+    )(*held)
 
 
 def solution(mesh):

time: 40.6 us -> 31.1 us (0.77)
  local copies, waits for them, and re-layouts: 4.72 us -> 0 us
  Pallas kernels: 35 us -> 30.3 us
    unnamed x10 -> x0, local copies, waits for them, and re-layouts: 4.72 us -> none
    pallas_call x1, Pallas kernels: 5.89 us -> 3.48 us  [body(): pl.pallas_call(update_kernel, grid=(rows // tile,), out_shape=like, in_sp...]
    pallas_call x1, Pallas kernels: 29.1 us -> 26.8 us  [body(): pl.pallas_call(functools.partial(exchange_kernel, cell_n, spot_n, rows *...]
where the time goes in v2:
time: 31.1 us; the launch traced here: 30.9 us
  Pallas kernels  30.3 us (97%)
  between operations  0.64 us (2%)
    pallas_call x1, Pallas kernels, body(): pl.pallas_call(functools.partial(exchange_kernel, cell_n, spot_n, rows *...  26.8 us
    pallas_call x1, Pallas kernels, body(): pl.pallas_call(update_kernel, grid=(rows // tile,), out_shape=like, in_sp...  3.48 us

profile of v2, /device:TPU:0, one launch (start us, length us, event | category | flops | bytes accessed | tf_op | source)
XLA Modules:
  0.0 30.9 jit_solution(7747154063555151278)
XLA Ops:
  0.6 26.8 %exchange.1 = (f32[1024,512]{1,0:T(8,128)S(1)}, bf16[1024,512]{1,0:T(8,128)(2,1)S(1)}, bf16[1024,512]{1,0:T(8,128)(2,1)S(1)}, f32[1024,512]{1,0:T(8,128)S(1)}, f...) custom-call(f32[1024,512]{1,0:T(8,128)} %logits_hbm.1, bf16[1024,128]{1,0:T(8,128)(2,1)} %expr_hbm.1, f32[512,128]{1,0:T(8,128)} %target_hbm.1, ...), custom_call_target="tpu_custom_call" | custom-call | flops 268435456 | bytes 16777216 | tf_op jit(solution)/shard_map/exchange/pallas_call | solution.py:246
  27.4 3.5 %update.1 = (f32[1024,512]{1,0:T(8,128)}, bf16[1024,512]{1,0:T(8,128)(2,1)}, bf16[1024,512]{1,0:T(8,128)(2,1)}) custom-call(f32[1024,512]{1,0:T(8,128)S(1)} %get-tuple-element.9.logits, bf16[1024,512]{1,0:T(8,128)(2,1)S(1)} %get-tuple-element.10.first, bf16[1024,512]{1,0:T(8,128)(2,1)S(1)} %get-tuple-element.11.second, ...), custom_call_target="tpu_custom_call" | custom-call | tf_op jit(solution)/shard_map/update/pallas_call | solution.py:283

commit v3 on v2

--- a/solution.py
+++ b/solution.py
@@ -40,10 +40,9 @@
     logits_hbm, expr_hbm, target_hbm, first_hbm, second_hbm,
     logits, first, second, probs, prob_grads, row_dots,
     expr, target, weights, expr_t, target_t, own_part, part,
-    stat_mine, stat_peer, part_peer, spot_mine, spot_peer, gene_mine, gene_peer,
-    grads, dots_mine, dots_peer,
-    load_sem, stat_send, stat_recv, part_send, part_recv, sums_send, sums_recv,
-    gene_send, gene_recv, grad_send, grad_recv, dots_send, dots_recv,
+    stat_mine, stat_peer, part_peer, gene_mine, gene_peer, shared, grads, dots_mine, dots_peer,
+    load_sem, stat_send, stat_recv, part_send, part_recv,
+    gene_send, gene_recv, shared_send, shared_recv, dots_send, dots_recv,
 ):
     rows, width = logits.shape
     genes = expr.shape[1]
@@ -70,13 +69,16 @@
     loads.append(pltpu.make_async_copy(target_hbm, target, load_sem.at[chunks + 1]))
     loads.append(pltpu.make_async_copy(first_hbm, first, load_sem.at[chunks + 2]))
     loads.append(pltpu.make_async_copy(second_hbm, second, load_sem.at[chunks + 3]))
-    for load in loads:
+    for load in loads[: chunks + 2]:
         load.start()
+    others = [(a, k) for k in range(spot_n) for a in range(cell_n) if a or k]
+
+    def other(a, k):
+        return (lax.rem(my_cell + a, cell_n), lax.rem(my_spot + k, spot_n))
+
     barrier = pltpu.get_barrier_semaphore()
-    for k in range(1, cell_n):
-        pl.semaphore_signal(barrier, inc=1, device_id=cell_peer(k), device_id_type=MESH)
-    for k in range(1, spot_n):
-        pl.semaphore_signal(barrier, inc=1, device_id=spot_peer_id(k), device_id_type=MESH)
+    for a, k in others:
+        pl.semaphore_signal(barrier, inc=1, device_id=other(a, k), device_id_type=MESH)
 
     mask = eye_mask()
 
@@ -91,7 +93,7 @@
             jnp.sum(expo, axis=1, keepdims=True), mask
         )
 
-    pl.semaphore_wait(barrier, cell_n + spot_n - 2)
+    pl.semaphore_wait(barrier, len(others))
 
     def send(src, dst, send_sem, recv_sem, device):
         copy = pltpu.make_async_remote_copy(
@@ -105,6 +107,8 @@
         send(stat_mine, stat_peer.at[k - 1], stat_send.at[k - 1], stat_recv.at[k - 1], spot_peer_id(k))
         for k in range(1, spot_n)
     ]
+    loads[chunks + 2].start()
+    loads[chunks + 3].start()
     loads[chunks].wait()
     loads[chunks + 1].wait()
     expr_t[...] = expr[...].astype(jnp.float32).T.astype(jnp.bfloat16)
@@ -144,47 +148,42 @@
     for k in range(cell_n - 1):
         predicted = predicted + part_peer[k].astype(jnp.float32)
 
-    product = predicted * own_target
-    square = predicted * predicted
-    spot_mine[0:1, :] = jnp.sum(product, axis=0, keepdims=True)
-    spot_mine[1:2, :] = jnp.sum(square, axis=0, keepdims=True)
-    spot_copies = [
-        send(spot_mine, spot_peer.at[k - 1], sums_send.at[k - 1], sums_recv.at[k - 1], cell_peer(k))
+    shared[my_cell] = predicted.astype(shared.dtype)
+    shared_copies = [
+        send(shared.at[my_cell], shared.at[my_cell], shared_send.at[k - 1], shared_recv.at[k - 1],
+             cell_peer(k))
         for k in range(1, cell_n)
     ]
-    gene_mine[0:1, :] = to_row(jnp.sum(product, axis=1, keepdims=True), mask)
-    gene_mine[1:2, :] = to_row(jnp.sum(square, axis=1, keepdims=True), mask)
+    gene_mine[0:1, :] = to_row(jnp.sum(predicted * own_target, axis=1, keepdims=True), mask)
+    gene_mine[1:2, :] = to_row(jnp.sum(predicted * predicted, axis=1, keepdims=True), mask)
     gene_copies = [
-        send(gene_mine, gene_peer.at[k - 1], gene_send.at[k - 1], gene_recv.at[k - 1], spot_peer_id(k))
-        for k in range(1, spot_n)
-    ]
+        send(gene_mine, gene_peer.at[my_cell, k], gene_send.at[a, k], gene_recv.at[a, k], other(a, k))
+        for a, k in others
+    ]
+    gene_peer[my_cell, 0] = gene_mine[...]
+    for copy in shared_copies:
+        copy.wait()
+    predicted = shared[...].astype(jnp.float32).reshape(genes, width)
+    wanted = target_t[...].reshape(genes, width)
+    spot_dot = jnp.sum(predicted * wanted, axis=0, keepdims=True)
+    spot_pred = jnp.sum(predicted * predicted, axis=0, keepdims=True)
+    spot_scale = lax.rsqrt((spot_pred + norm_epsilon) * (spot_target + norm_epsilon))
+    spot_lean = spot_dot / (spot_pred + norm_epsilon)
+    by_spot = (wanted - spot_lean * predicted) * spot_scale
     for copy in gene_copies:
         copy.wait()
-    gene_sums = gene_mine[...]
-    for k in range(spot_n - 1):
-        gene_sums = gene_sums + gene_peer[k]
-    gene_scale = lax.rsqrt((gene_sums[1:2] + norm_epsilon) * (gene_sums[2:3] + norm_epsilon))
-    gene_lean = gene_sums[0:1] / (gene_sums[1:2] + norm_epsilon)
-    gene_scale = to_column(gene_scale, mask, own_genes)
-    gene_lean = to_column(gene_lean, mask, own_genes)
-    by_gene = (own_target - gene_lean * predicted) * gene_scale
-    for copy in spot_copies:
-        copy.wait()
-    spot_sums = spot_mine[...]
-    for k in range(cell_n - 1):
-        spot_sums = spot_sums + spot_peer[k]
-    spot_scale = lax.rsqrt((spot_sums[1:2] + norm_epsilon) * (spot_target + norm_epsilon))
-    spot_lean = spot_sums[0:1] / (spot_sums[1:2] + norm_epsilon)
-    by_spot = (own_target - spot_lean * predicted) * spot_scale
-    grad = -loss_weight * (by_spot + ratio * by_gene)
-    grads[my_cell] = grad.astype(jnp.bfloat16)
-    grad_copies = [
-        send(grads.at[my_cell], grads.at[my_cell], grad_send.at[k - 1], grad_recv.at[k - 1], cell_peer(k))
-        for k in range(1, cell_n)
-    ]
-    for copy in grad_copies:
-        copy.wait()
-    grad_all = grads[...].reshape(genes, width)
+    for c in range(cell_n):
+        span = slice(c * own_genes, (c + 1) * own_genes)
+        gene_sums = gene_peer[c, 0]
+        for k in range(1, spot_n):
+            gene_sums = gene_sums + gene_peer[c, k]
+        gene_scale = lax.rsqrt((gene_sums[1:2] + norm_epsilon) * (gene_sums[2:3] + norm_epsilon))
+        gene_lean = gene_sums[0:1] / (gene_sums[1:2] + norm_epsilon)
+        gene_scale = to_column(gene_scale, mask, own_genes)
+        gene_lean = to_column(gene_lean, mask, own_genes)
+        by_gene = (wanted[span] - gene_lean * predicted[span]) * gene_scale
+        grads[span, :] = (-loss_weight * (by_spot[span] + ratio * by_gene)).astype(jnp.bfloat16)
+    grad_all = grads[...]
     for i in range(chunks):
         part_rows = slice(i * LANES, (i + 1) * LANES)
         prob_grad = jnp.dot(expr[part_rows, :], grad_all, preferred_element_type=jnp.float32)
@@ -225,7 +224,7 @@
         )
         first_hat = first_new * (learn_rate / (1.0 - beta_one**adam_count))
         second_hat = second_new * (1.0 / (1.0 - beta_two**adam_count))
-        new_logits[span, :] = logits[rows, :] - first_hat / (jnp.sqrt(second_hat) + adam_epsilon)
+        new_logits[span, :] = logits[rows, :] - first_hat / (second_hat * lax.rsqrt(second_hat) + adam_epsilon)
         new_first[span, :] = first_new.astype(jnp.bfloat16)
         new_second[span, :] = second_new.astype(jnp.bfloat16)
 
@@ -241,6 +240,7 @@
     in_vmem = pl.BlockSpec(memory_space=pltpu.VMEM)
     cell_sem = dma((cell_n - 1,))
     spot_sem = dma((spot_n - 1,))
+    all_sem = dma((cell_n, spot_n))
     like = [jax.ShapeDtypeStruct(x.shape, x.dtype) for x in (logits, first_moment, second_moment)]
     operands = (logits, cell_expr, spot_expr, first_moment, second_moment)
     held = pl.pallas_call(
@@ -259,16 +259,15 @@
             pltpu.VMEM((2 * chunks, LANES), f32),
             pltpu.VMEM((spot_n - 1, 2 * chunks, LANES), f32),
             pltpu.VMEM((cell_n - 1, own_genes, width), WIRE),
-            pltpu.VMEM((2, width), f32),
-            pltpu.VMEM((cell_n - 1, 2, width), f32),
             pltpu.VMEM((3, LANES), f32),
-            pltpu.VMEM((spot_n - 1, 3, LANES), f32),
-            pltpu.VMEM((cell_n, own_genes, width), jnp.bfloat16),
+            pltpu.VMEM((cell_n, spot_n, 3, LANES), f32),
+            pltpu.VMEM((cell_n, own_genes, width), WIRE),
+            pltpu.VMEM((genes, width), jnp.bfloat16),
             pltpu.VMEM((chunks, LANES), f32),
             pltpu.VMEM((spot_n - 1, chunks, LANES), f32),
             dma((chunks + 4,)),
-            spot_sem, spot_sem, cell_sem, cell_sem, cell_sem, cell_sem,
-            spot_sem, spot_sem, cell_sem, cell_sem, spot_sem, spot_sem,
+            spot_sem, spot_sem, cell_sem, cell_sem,
+            all_sem, all_sem, cell_sem, cell_sem, spot_sem, spot_sem,
         ],
         compiler_params=pltpu.CompilerParams(
             collective_id=0, has_side_effects=True, vmem_limit_bytes=24 << 20

time: 31.1 us -> 29.7 us (0.955)
  Pallas kernels: 30.3 us -> 28.9 us
    pallas_call x1, Pallas kernels: 26.8 us -> 25.7 us  [body(): pl.pallas_call(functools.partial(exchange_kernel, cell_n, spot_n, rows *...]
where the time goes in v3:
time: 29.7 us; the launch traced here: 29.6 us
  Pallas kernels  28.9 us (97%)
  between operations  0.64 us (2%)
    pallas_call x1, Pallas kernels, body(): pl.pallas_call(functools.partial(exchange_kernel, cell_n, spot_n, rows *...  25.7 us
    pallas_call x1, Pallas kernels, body(): pl.pallas_call(update_kernel, grid=(rows // tile,), out_shape=like, in_sp...  3.22 us

profile of v3, /device:TPU:0, one launch (start us, length us, event | category | flops | bytes accessed | tf_op | source)
XLA Modules:
  0.0 29.6 jit_solution(309277395493666029)
XLA Ops:
  0.6 25.7 %exchange.1 = (f32[1024,512]{1,0:T(8,128)S(1)}, bf16[1024,512]{1,0:T(8,128)(2,1)S(1)}, bf16[1024,512]{1,0:T(8,128)(2,1)S(1)}, f32[1024,512]{1,0:T(8,128)S(1)}, f...) custom-call(f32[1024,512]{1,0:T(8,128)} %logits_hbm.1, bf16[1024,128]{1,0:T(8,128)(2,1)} %expr_hbm.1, f32[512,128]{1,0:T(8,128)} %target_hbm.1, ...), custom_call_target="tpu_custom_call" | custom-call | flops 268435456 | bytes 16777216 | tf_op jit(solution)/shard_map/exchange/pallas_call | solution.py:246
  26.4 3.2 %update.1 = (f32[1024,512]{1,0:T(8,128)}, bf16[1024,512]{1,0:T(8,128)(2,1)}, bf16[1024,512]{1,0:T(8,128)(2,1)}) custom-call(f32[1024,512]{1,0:T(8,128)S(1)} %get-tuple-element.9.logits, bf16[1024,512]{1,0:T(8,128)(2,1)S(1)} %get-tuple-element.10.first, bf16[1024,512]{1,0:T(8,128)(2,1)S(1)} %get-tuple-element.11.second, ...), custom_call_target="tpu_custom_call" | custom-call | tf_op jit(solution)/shard_map/update/pallas_call | solution.py:282

commit v4 on v3

--- a/solution.py
+++ b/solution.py
@@ -39,7 +39,7 @@
     cell_n, spot_n, cells, spots,
     logits_hbm, expr_hbm, target_hbm, first_hbm, second_hbm,
     logits, first, second, probs, prob_grads, row_dots,
-    expr, target, weights, expr_t, target_t, own_part, part,
+    first_in, second_in, expr, target, weights, expr_t, target_t, own_part, part,
     stat_mine, stat_peer, part_peer, gene_mine, gene_peer, shared, grads, dots_mine, dots_peer,
     load_sem, stat_send, stat_recv, part_send, part_recv,
     gene_send, gene_recv, shared_send, shared_recv, dots_send, dots_recv,
@@ -67,11 +67,11 @@
     ]
     loads.append(pltpu.make_async_copy(expr_hbm, expr, load_sem.at[chunks]))
     loads.append(pltpu.make_async_copy(target_hbm, target, load_sem.at[chunks + 1]))
-    loads.append(pltpu.make_async_copy(first_hbm, first, load_sem.at[chunks + 2]))
-    loads.append(pltpu.make_async_copy(second_hbm, second, load_sem.at[chunks + 3]))
+    loads.append(pltpu.make_async_copy(first_hbm, first_in, load_sem.at[chunks + 2]))
+    loads.append(pltpu.make_async_copy(second_hbm, second_in, load_sem.at[chunks + 3]))
     for load in loads[: chunks + 2]:
         load.start()
-    others = [(a, k) for k in range(spot_n) for a in range(cell_n) if a or k]
+    others = [(a, k) for k in range(spot_n) for a in range(cell_n) if a or k][::-1]
 
     def other(a, k):
         return (lax.rem(my_cell + a, cell_n), lax.rem(my_spot + k, spot_n))
@@ -149,16 +149,16 @@
         predicted = predicted + part_peer[k].astype(jnp.float32)
 
     shared[my_cell] = predicted.astype(shared.dtype)
-    shared_copies = [
-        send(shared.at[my_cell], shared.at[my_cell], shared_send.at[k - 1], shared_recv.at[k - 1],
-             cell_peer(k))
-        for k in range(1, cell_n)
-    ]
     gene_mine[0:1, :] = to_row(jnp.sum(predicted * own_target, axis=1, keepdims=True), mask)
     gene_mine[1:2, :] = to_row(jnp.sum(predicted * predicted, axis=1, keepdims=True), mask)
     gene_copies = [
         send(gene_mine, gene_peer.at[my_cell, k], gene_send.at[a, k], gene_recv.at[a, k], other(a, k))
         for a, k in others
+    ]
+    shared_copies = [
+        send(shared.at[my_cell], shared.at[my_cell], shared_send.at[k - 1], shared_recv.at[k - 1],
+             cell_peer(k))
+        for k in range(1, cell_n)
     ]
     gene_peer[my_cell, 0] = gene_mine[...]
     for copy in shared_copies:
@@ -197,6 +197,10 @@
     ]
     loads[chunks + 2].wait()
     loads[chunks + 3].wait()
+    for i in range(chunks):
+        part_rows = slice(i * LANES, (i + 1) * LANES)
+        first[part_rows, :] = beta_one * first_in[part_rows, :].astype(jnp.float32)
+        second[part_rows, :] = beta_two * second_in[part_rows, :].astype(jnp.float32)
     for copy in dots_copies:
         copy.wait()
     row_dot = dots_mine[...]
@@ -206,27 +210,32 @@
 
 
 def update_kernel(
-    logits, first, second, probs, prob_grads, row_dots, new_logits, new_first, new_second
+    logits, first, second, probs, prob_grads, row_dots,
+    logits_hbm, first_hbm, second_hbm,
+    new_logits, new_first, new_second, store_sem,
 ):
-    at = pl.program_id(0)
     mask = eye_mask()
-    per = new_logits.shape[0] // LANES
-    for j in range(per):
-        span = slice(j * LANES, (j + 1) * LANES)
-        row = at * per + j
-        rows = pl.ds(pl.multiple_of(row * LANES, LANES), LANES)
-        row_dot = to_column(row_dots[pl.ds(row, 1), :], mask)
-        logit_grad = probs[rows, :] * (prob_grads[rows, :] - row_dot)
-        first_new = beta_one * first[rows, :].astype(jnp.float32) + (1.0 - beta_one) * logit_grad
-        second_new = (
-            beta_two * second[rows, :].astype(jnp.float32)
-            + (1.0 - beta_two) * logit_grad * logit_grad
-        )
+    stores = []
+    for i in range(row_dots.shape[0]):
+        span = pl.ds(i * LANES, LANES)
+        row_dot = to_column(row_dots[i : i + 1, :], mask)
+        logit_grad = probs[span, :] * (prob_grads[span, :] - row_dot)
+        first_new = first[span, :] + (1.0 - beta_one) * logit_grad
+        second_new = second[span, :] + (1.0 - beta_two) * logit_grad * logit_grad
         first_hat = first_new * (learn_rate / (1.0 - beta_one**adam_count))
         second_hat = second_new * (1.0 / (1.0 - beta_two**adam_count))
-        new_logits[span, :] = logits[rows, :] - first_hat / (second_hat * lax.rsqrt(second_hat) + adam_epsilon)
+        new_logits[span, :] = logits[span, :] - first_hat / (
+            second_hat * lax.rsqrt(second_hat) + adam_epsilon
+        )
         new_first[span, :] = first_new.astype(jnp.bfloat16)
         new_second[span, :] = second_new.astype(jnp.bfloat16)
+        pairs = ((new_logits, logits_hbm), (new_first, first_hbm), (new_second, second_hbm))
+        for j, (held, out) in enumerate(pairs):
+            copy = pltpu.make_async_copy(held.at[span], out.at[span], store_sem.at[i, j])
+            copy.start()
+            stores.append(copy)
+    for copy in stores:
+        copy.wait()
 
 
 def body(cell_n, spot_n, logits, first_moment, second_moment, cell_expr, spot_expr):
@@ -245,10 +254,12 @@
     operands = (logits, cell_expr, spot_expr, first_moment, second_moment)
     held = pl.pallas_call(
         functools.partial(exchange_kernel, cell_n, spot_n, rows * cell_n, width * spot_n),
-        out_shape=(*like, like[0], like[0], jax.ShapeDtypeStruct((chunks, LANES), f32)),
+        out_shape=(*like[:1] * 5, jax.ShapeDtypeStruct((chunks, LANES), f32)),
         in_specs=[in_hbm] * 5,
         out_specs=(in_vmem,) * 6,
         scratch_shapes=[
+            pltpu.VMEM((rows, width), jnp.bfloat16),
+            pltpu.VMEM((rows, width), jnp.bfloat16),
             pltpu.VMEM((rows, genes), jnp.bfloat16),
             pltpu.VMEM((width, genes), f32),
             pltpu.VMEM((rows, width), jnp.bfloat16),
@@ -277,14 +288,12 @@
         ),
         name="exchange",
     )(*(pltpu.with_memory_space_constraint(x, pltpu.HBM) for x in operands))
-    tile = 2 * LANES if rows % (2 * LANES) == 0 else LANES
-    by_row = pl.BlockSpec((tile, width), lambda i: (i, 0))
     return pl.pallas_call(
         update_kernel,
-        grid=(rows // tile,),
         out_shape=like,
         in_specs=[in_vmem] * 6,
-        out_specs=(by_row, by_row, by_row),
+        out_specs=(in_hbm,) * 3,
+        scratch_shapes=[pltpu.VMEM(x.shape, x.dtype) for x in like] + [dma((chunks, 3))],
         compiler_params=pltpu.CompilerParams(vmem_limit_bytes=16 << 20),
         name="update",
     )(*held)

time: 29.7 us -> 28.7 us (0.966)
  Pallas kernels: 28.9 us -> 27.9 us
    pallas_call x1, Pallas kernels: 3.22 us -> 2.48 us  [body(): pl.pallas_call(update_kernel, out_shape=like, in_specs=[in_vmem] * 6, out...]
where the time goes in v4:
time: 28.7 us; the launch traced here: 28.6 us
  Pallas kernels  27.9 us (97%)
  between operations  0.64 us (2%)
    pallas_call x1, Pallas kernels, body(): pl.pallas_call(functools.partial(exchange_kernel, cell_n, spot_n, rows *...  25.5 us
    pallas_call x1, Pallas kernels, body(): pl.pallas_call(update_kernel, out_shape=like, in_specs=[in_vmem] * 6, out...  2.48 us

profile of v4, /device:TPU:0, one launch (start us, length us, event | category | flops | bytes accessed | tf_op | source)
XLA Modules:
  0.0 28.6 jit_solution(17783734463377294926)
XLA Ops:
  0.6 25.5 %exchange.1 = (f32[1024,512]{1,0:T(8,128)S(1)}, f32[1024,512]{1,0:T(8,128)S(1)}, f32[1024,512]{1,0:T(8,128)S(1)}, f32[1024,512]{1,0:T(8,128)S(1)}, f32[1024,512]{1,0:T(8,128)S(1)}, /*index=5*/f32[8,128]{1,0:T(8,128)S(1)}) custom-call(f32[1024,512]{1,0:T(8,128)} %logits_hbm.1, bf16[1024,128]{1,0:T(8,128)(2,1)} %expr_hbm.1, f32[512,128]{1,0:T(8,128)} %target_hbm.1, ...), custom_call_target="tpu_custom_call" | custom-call | flops 268435456 | bytes 16777216 | tf_op jit(solution)/shard_map/exchange/pallas_call | solution.py:255
  26.1 2.5 %update.1 = (f32[1024,512]{1,0:T(8,128)}, bf16[1024,512]{1,0:T(8,128)(2,1)}, bf16[1024,512]{1,0:T(8,128)(2,1)}) custom-call(f32[1024,512]{1,0:T(8,128)S(1)} %get-tuple-element.9.logits, f32[1024,512]{1,0:T(8,128)S(1)} %get-tuple-element.10.first, f32[1024,512]{1,0:T(8,128)S(1)} %get-tuple-element.11.second, f32[1024,512]{1,0:T(8,128)S(1)} %get-tuple-element.12.probs, ...), custom_call_target="tpu_custom_call" | custom-call | tf_op jit(solution)/shard_map/update/pallas_call | solution.py:291

commit v5 on v4

--- a/solution.py
+++ b/solution.py
@@ -105,7 +105,7 @@
 
     stat_copies = [
         send(stat_mine, stat_peer.at[k - 1], stat_send.at[k - 1], stat_recv.at[k - 1], spot_peer_id(k))
-        for k in range(1, spot_n)
+        for k in range(spot_n - 1, 0, -1)
     ]
     loads[chunks + 2].start()
     loads[chunks + 3].start()
@@ -193,7 +193,7 @@
         )
     dots_copies = [
         send(dots_mine, dots_peer.at[k - 1], dots_send.at[k - 1], dots_recv.at[k - 1], spot_peer_id(k))
-        for k in range(1, spot_n)
+        for k in range(spot_n - 1, 0, -1)
     ]
     loads[chunks + 2].wait()
     loads[chunks + 3].wait()

time: 28.7 us -> 28 us (0.976)
  Pallas kernels: 27.9 us -> 27.2 us
    pallas_call x1, Pallas kernels: 25.5 us -> 24.8 us  [body(): pl.pallas_call(functools.partial(exchange_kernel, cell_n, spot_n, rows *...]
where the time goes in v5:
time: 28 us; the launch traced here: 27.9 us
  Pallas kernels  27.2 us (97%)
  between operations  0.64 us (2%)
    pallas_call x1, Pallas kernels, body(): pl.pallas_call(functools.partial(exchange_kernel, cell_n, spot_n, rows *...  24.8 us
    pallas_call x1, Pallas kernels, body(): pl.pallas_call(update_kernel, out_shape=like, in_specs=[in_vmem] * 6, out...  2.48 us

profile of v5, /device:TPU:0, one launch (start us, length us, event | category | flops | bytes accessed | tf_op | source)
XLA Modules:
  0.0 27.9 jit_solution(17559976117593092748)
XLA Ops:
  0.6 24.8 %exchange.1 = (f32[1024,512]{1,0:T(8,128)S(1)}, f32[1024,512]{1,0:T(8,128)S(1)}, f32[1024,512]{1,0:T(8,128)S(1)}, f32[1024,512]{1,0:T(8,128)S(1)}, f32[1024,512]{1,0:T(8,128)S(1)}, /*index=5*/f32[8,128]{1,0:T(8,128)S(1)}) custom-call(f32[1024,512]{1,0:T(8,128)} %logits_hbm.1, bf16[1024,128]{1,0:T(8,128)(2,1)} %expr_hbm.1, f32[512,128]{1,0:T(8,128)} %target_hbm.1, ...), custom_call_target="tpu_custom_call" | custom-call | flops 268435456 | bytes 16777216 | tf_op jit(solution)/shard_map/exchange/pallas_call | solution.py:255
  25.4 2.5 %update.1 = (f32[1024,512]{1,0:T(8,128)}, bf16[1024,512]{1,0:T(8,128)(2,1)}, bf16[1024,512]{1,0:T(8,128)(2,1)}) custom-call(f32[1024,512]{1,0:T(8,128)S(1)} %get-tuple-element.9.logits, f32[1024,512]{1,0:T(8,128)S(1)} %get-tuple-element.10.first, f32[1024,512]{1,0:T(8,128)S(1)} %get-tuple-element.11.second, f32[1024,512]{1,0:T(8,128)S(1)} %get-tuple-element.12.probs, ...), custom_call_target="tpu_custom_call" | custom-call | tf_op jit(solution)/shard_map/update/pallas_call | solution.py:291
